TPU v7x, 128 devices: a whole 4x4x4 slice. The times are simulated.
128 devices in a mesh: dev: 128 (over x, y, z, core).
Axes of the slice: x: 4, y: 4, z: 4, core: 2. Of those that a mesh axis runs over, the one named last changes fastest.
Arguments:
- density: bfloat16 [1024, 262144], P('dev'), may hold values from -6 to 6
- flags: int32 [1024], P('dev'), may hold values 0 or 1
- courant: float32 [1024], P('dev'), may hold values from 0.1 to 0.9
- spectral: bfloat16 [1024, 1024], replicated, may hold values from -0.1875 to 0.1875
- tensor: bfloat16 [128, 1024, 1024], P('dev'), may hold values from -0.1875 to 0.1875
- owner: int32 [4], replicated, may hold values from 0 to 127, as said below
Outputs:
- coeffs: bfloat16 [1024, 262144], P(None, 'dev')
- collision: float32 [4, 262144], P(None, 'dev')
Inputs may be any that keep to these rules, and one draw needn't show every extreme that they name: `owner`: distinct slice indices, one of which is 127.
All inputs are finite; a program needn't handle non-finite values. No bound on the sum of `flags` on one device may be relied on, other than what follows from the above.
Results may differ from a plain program's by a relative error of at most 0.0064.
Values may be sent and summed in bfloat16 or wider, within the bound.
No kernel may reach another device: no remote copies, remote signals or barrier semaphores. Data moves between devices by JAX's collectives and lax.ppermute only.
A program may use at most 128 MiB of HBM per device.

v0:
```python
import math

import jax
import jax.numpy as jnp
from jax import lax
from jax.sharding import PartitionSpec as P


def spread(x, axis, root):
    mine = lax.axis_index(axis) == root
    return lax.psum(jnp.where(mine, x, jnp.zeros_like(x)), axis)


def upwind_step(field, neighbour, rate):
    return (field - rate * (field - neighbour)).astype(jnp.bfloat16)


def fetch_slice(tensor, owner, index):
    return spread(tensor[0], "dev", owner[index])


def local(density, flags, courant, spectral, tensor, owner):
    field = density.astype(jnp.float32)
    neighbour = jnp.where(
        flags[:, None] == 1, jnp.roll(field, 1, axis=1), jnp.roll(field, -1, axis=1)
    )
    moved = upwind_step(field, neighbour, courant[:, None])
    cell_block = lax.all_to_all(moved, "dev", split_axis=1, concat_axis=0, tiled=True)
    coeffs = jnp.dot(spectral, cell_block, preferred_element_type=jnp.float32).astype(jnp.bfloat16)
    factor = 1.0 / math.sqrt(spectral.shape[0])

    def quadratic(slab):
        image = jnp.dot(slab, coeffs, preferred_element_type=jnp.float32)
        return jnp.sum(coeffs * image, axis=0) * factor

    count = owner.shape[0]
    results = [quadratic(fetch_slice(tensor, owner, index)) for index in range(count)]
    return (coeffs, jnp.stack(results))


def solution(mesh):
    in_specs = (P("dev", None), P("dev"), P("dev"), P(), P("dev", None, None), P())
    out_specs = (P(None, "dev"), P(None, "dev"))
    return jax.shard_map(local, mesh=mesh, in_specs=in_specs, out_specs=out_specs, check_vma=False)
```

profile of v0, /device:TPU:1, one launch (start us, length us, event | category | flops | bytes accessed | tf_op | source)
XLA Modules:
  0.0 261.1 jit_solution(14438195279546008698)
XLA Ops:
  7.2 0.0 copy-start
  7.2 0.0 copy-start.1
  7.2 0.0 copy-start.7
  7.2 0.0 copy-start.3
  7.2 5.1 %fusion.13 = (f32[8,262143]{1,0:T(8,128)S(1)}, f32[8,262143]{1,0:T(8,128)S(1)}) fusion(bf16[8,262144]{1,0:T(8,128)(2,1)} %param.6), kind=kLoop, calls=%fused_computation.26 | loop fusion | bytes 33554304 | tf_op jit(solution)/shard_map/jit(_roll_static)/slice | solution.py:25
  12.3 0.0 copy-done.1
  12.3 0.1 fusion.14
  12.4 0.0 copy-done.7
  12.4 0.0 copy-done.3
  12.4 7.2 %fusion.7 = bf16[8,262144]{1,0:T(8,128)(2,1)} fusion(f32[8,262143]{1,0:T(8,128)S(1)} %get-tuple-element.7, f32[8,1]{1,0:T(8,128)S(1)} %get-tuple-element.9, f32[8,1]{1,0:T(8,128)S(1)} %get-tuple-element.8, f32[8,262143]{1,0:T(8,128)S(1)} %get-tuple-element.6, f32[8]{0:T(128)S(1)} %copy-done.3, pred[8]{0:T(512)(128)(4,1)S(1)} %broadcast_compare_fusion, ...), kind=kLoop, calls=%fused_computation.12 | loop fusion | flops 16777216 | bytes 25165864 | tf_op jit(solution)/shard_map/convert_element_type | solution.py:15
  19.6 0.0 copy-start.2
  19.6 12.0 %all-to-all-start = ((bf16[8,128,2048]{2,0,1:T(8,128)(2,1)}), bf16[8,128,2048]{2,0,1:T(8,128)(2,1)}, u32[]{:S(2)}, u32[]{:S(2)}) async-start(bf16[8,128,2048]{2,0,1:T(8,128)(2,1)} %bitcast.34), calls=%async_computation | async-start | bytes 8388608 | tf_op jit(solution)/shard_map/all_to_all | solution.py:28
  31.6 0.2 all-reduce.3.cloned.1.call-start
  31.8 0.0 copy-done.2
  31.8 0.6 fusion.15
  34.9 5.0 %select_bitcast_fusion.3 = (bf16[1024,1024]{1,0:T(8,128)(2,1)}, bf16[1024,1024]{1,0:T(8,128)(2,1)}, bf16[1024,1024]{1,0:T(8,128)(2,1)}, bf16[1024,1024]{1,0:T(8,128)(2,1)}) fusion(bf16[1,1024,1024]{2,1,0:T(8,128)(2,1)} %param.10, pred[]{:T(512)S(6)} %eq.17, pred[]{:T(512)S(6)} %eq.18, pred[]{:T(512)S(6)} %eq.20, pred[]{:T(512)S(6)} %eq.19), kind=kLoop, calls=%fused_computation.19 | loop fusion | flops 4194304 | bytes 10485764 | tf_op jit(solution)/shard_map/jit(_where)/select_n | solution.py:11
  39.9 0.0 all-reduce.3.cloned.1.call-update
  39.9 48.6 %all-to-all-done = bf16[8,128,2048]{2,0,1:T(8,128)(2,1)} async-done(((bf16[8,128,2048]{2,0,1:T(8,128)(2,1)}), bf16[8,128,2048]{2,0,1:T(8,128)(2,1)}, u32[]{:S(2)}, u32[]{:S(2)}) %all-to-all-start) | async-done | bytes 4194336 | tf_op jit(solution)/shard_map/all_to_all | solution.py:28
  88.5 0.0 copy-done
  88.5 8.3 %fusion.10 = bf16[2048,1024]{0,1:T(8,128)(2,1)} fusion(bf16[1024,1024]{1,0:T(8,128)(2,1)S(1)} %copy-done, bf16[8,128,2048]{2,0,1:T(8,128)(2,1)} %all-to-all-done), kind=kOutput, calls=%fused_computation.15 | convolution fusion | flops 4297064448 | bytes 10485760 | tf_op jit(solution)/shard_map/dot_general | solution.py:29
  96.9 133.6 %all-reduce.3.cloned.1.call-done = (bf16[1024,1024]{1,0:T(8,128)(2,1)}, bf16[1024,1024]{1,0:T(8,128)(2,1)}, bf16[1024,1024]{1,0:T(8,128)(2,1)}, bf16[1024,1024]{1,0:T(8,128)(2,1)}) async-done(((bf16[1024,1024]{1,0:T(8,128)(2,1)}, bf16[1024,1024]{1,0:T(8,128)(2,1)}, bf16[1024,1024]{1,0:T(8,128)(2,1)}, bf16[1024,1024]{1,0:T(8,128)(2,1)}), (bf16[1024,1024]{1,0:T(8,128)(2,1)}, bf16[1024,1024]{1,0:T(8,128)(2,1)}, ...) | async-done | bytes 8388624 | tf_op jit(solution)/shard_map/psum | solution.py:11
  230.5 8.7 %fusion.3 = f32[2048]{0:T(1024)S(1)} fusion(bf16[1024,2048]{1,0:T(8,128)(2,1)} %bitcast.39, bf16[1024,1024]{1,0:T(8,128)(2,1)} %get-tuple-element.2, bf16[2048,1024]{0,1:T(8,128)(2,1)} %fusion.10), kind=kOutput, calls=%fused_computation.7 | convolution fusion | flops 4301256704 | bytes 10493952 | tf_op jit(solution)/shard_map/dot_general | solution.py:33
  239.2 0.0 copy-done.6
  239.2 0.0 copy-done.8
  239.2 0.0 copy-start.5
  239.2 4.7 %fusion.2 = f32[2048]{0:T(1024)S(1)} fusion(bf16[1024,2048]{1,0:T(8,128)(2,1)S(1)} %bitcast.41, bf16[1024,1024]{1,0:T(8,128)(2,1)S(1)} %copy-done.6, bf16[2048,1024]{0,1:T(8,128)(2,1)S(1)} %copy-done.8), kind=kOutput, calls=%fused_computation.6 | convolution fusion | flops 4301256704 | bytes 10493952 | tf_op jit(solution)/shard_map/dot_general | solution.py:33
  244.0 0.0 copy-done.5
  244.0 0.0 copy-start.4
  244.0 4.8 %fusion.1 = f32[2048]{0:T(1024)S(1)} fusion(bf16[1024,2048]{1,0:T(8,128)(2,1)S(1)} %bitcast.42, bf16[1024,1024]{1,0:T(8,128)(2,1)S(1)} %copy-done.5, bf16[2048,1024]{0,1:T(8,128)(2,1)S(1)} %copy-done.8), kind=kOutput, calls=%fused_computation.5 | convolution fusion | flops 4301256704 | bytes 10493952 | tf_op jit(solution)/shard_map/dot_general | solution.py:33
  248.8 0.0 copy-done.4
  248.8 4.7 %fusion = f32[2048]{0:T(1024)S(1)} fusion(bf16[1024,2048]{1,0:T(8,128)(2,1)S(1)} %bitcast.43, bf16[1024,1024]{1,0:T(8,128)(2,1)S(1)} %copy-done.4, bf16[2048,1024]{0,1:T(8,128)(2,1)S(1)} %copy-done.8), kind=kOutput, calls=%fused_computation.4 | convolution fusion | flops 4301256704 | bytes 10493952 | tf_op jit(solution)/shard_map/dot_general | solution.py:33
  253.6 0.7 pad_maximum_fusion
  (7 shorter events, 0.0 us)
Async XLA Ops:
  7.2 81.4 %copy-start = (bf16[1024,1024]{1,0:T(8,128)(2,1)S(1)}, bf16[1024,1024]{1,0:T(8,128)(2,1)}, u32[]{:S(2)}) copy-start(bf16[1024,1024]{1,0:T(8,128)(2,1)} %param.9) | copy-start | bytes 6291460
  7.2 5.1 %copy-start.1 = (bf16[8,262144]{1,0:T(8,128)(2,1)S(1)}, bf16[8,262144]{1,0:T(8,128)(2,1)}, u32[]{:S(2)}) copy-start(bf16[8,262144]{1,0:T(8,128)(2,1)} %param.6) | copy-start | bytes 12582916
  7.2 5.2 %copy-start.7 = (s32[8]{0:T(128)S(1)}, s32[8]{0:T(128)}, u32[]{:S(2)}) copy-start(s32[8]{0:T(128)} %param.7) | copy-start | bytes 100
  7.2 5.2 %copy-start.3 = (f32[8]{0:T(128)S(1)}, f32[8]{0:T(128)}, u32[]{:S(2)}) copy-start(f32[8]{0:T(128)} %param.8) | copy-start | bytes 100
  19.6 12.2 %copy-start.2 = (s32[4]{0:T(128)S(1)}, s32[4]{0:T(128)}, u32[]{:S(2)}) copy-start(s32[4]{0:T(128)} %param.11) | copy-start | bytes 52
  19.6 68.9 %all-to-all-start = ((bf16[8,128,2048]{2,0,1:T(8,128)(2,1)}), bf16[8,128,2048]{2,0,1:T(8,128)(2,1)}, u32[]{:S(2)}, u32[]{:S(2)}) async-start(bf16[8,128,2048]{2,0,1:T(8,128)(2,1)} %bitcast.34), calls=%async_computation | async-start | bytes 8388608 | tf_op jit(solution)/shard_map/all_to_all | solution.py:28
  31.6 198.9 %all-reduce.3.cloned.1.call-start = ((), (), s32[]{:S(2)}) async-start(), calls=%async_computation.1 | async-start | bytes 16777216 | tf_op jit(solution)/shard_map/psum | solution.py:11
  230.5 8.7 %copy-start.6 = (bf16[1024,1024]{1,0:T(8,128)(2,1)S(1)}, bf16[1024,1024]{1,0:T(8,128)(2,1)}, u32[]{:S(2)}) copy-start(bf16[1024,1024]{1,0:T(8,128)(2,1)} %get-tuple-element.3) | copy-start | bytes 6291460
  230.5 8.7 %copy-start.8 = (bf16[2048,1024]{0,1:T(8,128)(2,1)S(1)}, bf16[2048,1024]{0,1:T(8,128)(2,1)}, u32[]{:S(2)}) copy-start(bf16[2048,1024]{0,1:T(8,128)(2,1)} %fusion.10) | copy-start | bytes 12582916
  239.2 4.8 %copy-start.5 = (bf16[1024,1024]{1,0:T(8,128)(2,1)S(1)}, bf16[1024,1024]{1,0:T(8,128)(2,1)}, u32[]{:S(2)}) copy-start(bf16[1024,1024]{1,0:T(8,128)(2,1)} %get-tuple-element.4) | copy-start | bytes 6291460
  244.0 4.8 %copy-start.4 = (bf16[1024,1024]{1,0:T(8,128)(2,1)S(1)}, bf16[1024,1024]{1,0:T(8,128)(2,1)}, u32[]{:S(2)}) copy-start(bf16[1024,1024]{1,0:T(8,128)(2,1)} %get-tuple-element.5) | copy-start | bytes 6291460
Sparse Core Ops, SparseCore 0:
  40.0 190.3 all-reduce.2
where the time goes:
time: 261 us
  waiting for transfers between devices  182 us (70%)
  matrix products  31.3 us (12%)
  between operations  16.7 us (6%)
  other arithmetic  12.9 us (5%)
  starting transfers between devices  12.2 us (5%)
  local copies, waits for them, and re-layouts  5.82 us (2%)
    psum x1, waiting for transfers between devices, spread(): return lax.psum(jnp.where(mine, x, jnp.zeros_like(x)), axis)  134 us
    all_to_all x1, waiting for transfers between devices, local(): lax.all_to_all(moved, 'dev', split_axis=1, concat_axis=0, tiled=True)  48.6 us
    dot_general x4, matrix products, quadratic(): image = jnp.dot(slab, coeffs, preferred_element_type=jnp.float32)  22.9 us
    all_to_all x1, starting transfers between devices, local(): lax.all_to_all(moved, 'dev', split_axis=1, concat_axis=0, tiled=True)  12 us
    dot_general x1, matrix products, local(): jnp.dot(spectral, cell_block, preferred_element_type=jnp.float32)  8.31 us
    convert_element_type x1, other arithmetic, upwind_step(): return (field - rate * (field - neighbour)).astype(jnp.bfloat16)  7.23 us
  transfers between devices with their start and end apart: 2, of which 2 were waited for; matrix products, arithmetic and copies ran while one was open for 5% of the time, Pallas kernels for 0%

commit v1 on v0

v1 whole, which is shorter than its diff:
```python
import math

import jax
import jax.numpy as jnp
from jax import lax
from jax.experimental import pallas as pl
from jax.experimental.pallas import tpu as pltpu
from jax.sharding import PartitionSpec as P

BLOCK = 256
LANES = 128
GROUP = 8


def fold_pairs(count):
    return [(i, j) for i in range(count) for j in range(i, count)]


def fold_kernel(t_ref, u_ref):
    count = t_ref.shape[1] // BLOCK
    for at, (i, j) in enumerate(fold_pairs(count)):
        rows, cols = pl.ds(i * BLOCK, BLOCK), pl.ds(j * BLOCK, BLOCK)
        block = t_ref[0, rows, cols]
        if i != j:
            mirror = t_ref[0, cols, rows].astype(jnp.float32).T
            block = (block.astype(jnp.float32) + mirror).astype(jnp.bfloat16)
        for half in range(BLOCK // LANES):
            start = (at * (BLOCK // LANES) + half) * BLOCK
            u_ref[pl.ds(start, BLOCK), :] = block[:, half * LANES : (half + 1) * LANES]


def fold(tensor):
    size = tensor.shape[1]
    rows = len(fold_pairs(size // BLOCK)) * BLOCK * (BLOCK // LANES)
    return pl.pallas_call(
        fold_kernel,
        out_shape=jax.ShapeDtypeStruct((rows, LANES), jnp.bfloat16),
        in_specs=[pl.BlockSpec(memory_space=pltpu.VMEM)],
        out_specs=pl.BlockSpec(memory_space=pltpu.VMEM),
        compiler_params=pltpu.CompilerParams(vmem_limit_bytes=24 << 20),
        cost_estimate=pl.CostEstimate(flops=2 * size * size, bytes_accessed=4 * size * size, transcendentals=0),
        name="fold",
    )(tensor)


def advect_kernel(flags_ref, courant_ref, before_ref, here_ref, after_ref, out_ref):
    nodes, width = out_ref.shape[1], out_ref.shape[2]
    row = lax.broadcasted_iota(jnp.int32, (nodes, 1), 0)
    flag = jnp.zeros((nodes, 1), jnp.int32)
    rate = jnp.zeros((nodes, 1), jnp.float32)
    for r in range(nodes):
        flag = jnp.where(row == r, flags_ref[r], flag)
        rate = jnp.where(row == r, courant_ref[r], rate)
    upward = jnp.broadcast_to(flag, (nodes, width)) == 1
    for d in range(out_ref.shape[0]):
        start, stop = d * width, (d + 1) * width
        last = d == out_ref.shape[0] - 1
        before = before_ref[...] if d == 0 else here_ref[:, start - LANES : start]
        after = after_ref[...] if last else here_ref[:, stop : stop + LANES]
        field = here_ref[:, start:stop].astype(jnp.float32)
        line = jnp.concatenate([before.astype(jnp.float32), field, after.astype(jnp.float32)], axis=1)
        left = pltpu.roll(line, 1, axis=1)[:, LANES : LANES + width]
        right = pltpu.roll(line, width + 2 * LANES - 1, axis=1)[:, LANES : LANES + width]
        neighbour = jnp.where(upward, left, right)
        out_ref[d] = (field - rate * (field - neighbour)).astype(jnp.bfloat16)


def advect(density, flags, courant, parts):
    nodes, cells = density.shape
    width = cells // parts
    wide = GROUP * width // LANES
    lines = cells // LANES
    return pl.pallas_call(
        advect_kernel,
        grid=(parts // GROUP,),
        out_shape=jax.ShapeDtypeStruct((parts, nodes, width), jnp.bfloat16),
        in_specs=[
            pl.BlockSpec(memory_space=pltpu.SMEM),
            pl.BlockSpec(memory_space=pltpu.SMEM),
            pl.BlockSpec((nodes, LANES), lambda i: (0, (i * wide + lines - 1) % lines)),
            pl.BlockSpec((nodes, GROUP * width), lambda i: (0, i)),
            pl.BlockSpec((nodes, LANES), lambda i: (0, ((i + 1) * wide) % lines)),
        ],
        out_specs=pl.BlockSpec((GROUP, nodes, width), lambda i: (i, 0, 0)),
        compiler_params=pltpu.CompilerParams(vmem_limit_bytes=24 << 20),
        cost_estimate=pl.CostEstimate(flops=4 * nodes * cells, bytes_accessed=4 * nodes * cells, transcendentals=0),
        name="advect",
    )(flags, courant, density, density, density)


def transform_kernel(s_ref, x_ref, c_ref):
    c_ref[...] = jnp.dot(s_ref[...], x_ref[...], preferred_element_type=jnp.float32).astype(jnp.bfloat16)


def transform(spectral, block, tile=512):
    size, width = spectral.shape[0], block.shape[1]
    return pl.pallas_call(
        transform_kernel,
        grid=(width // tile,),
        out_shape=jax.ShapeDtypeStruct((size, width), jnp.bfloat16),
        in_specs=[
            pl.BlockSpec(spectral.shape, lambda i: (0, 0)),
            pl.BlockSpec((block.shape[0], tile), lambda i: (0, i)),
        ],
        out_specs=pl.BlockSpec((size, tile), lambda i: (0, i)),
        compiler_params=pltpu.CompilerParams(vmem_limit_bytes=32 << 20),
        cost_estimate=pl.CostEstimate(
            flops=2 * size * block.shape[0] * width, bytes_accessed=6 * size * width, transcendentals=0
        ),
        name="transform",
    )(spectral, block)


def quadratic_kernel(u_hbm, c_ref, out_ref, u_ref, sems):
    size, tile = c_ref.shape
    count = size // BLOCK
    slots = out_ref.shape[0]
    pairs = fold_pairs(count)
    halves = BLOCK // LANES
    first = pl.program_id(0) == 0
    copies = [pltpu.make_async_copy(u_hbm.at[:, m], u_ref.at[m], sems.at[m]) for m in range(slots)]

    @pl.when(first)
    def _():
        for copy in copies:
            copy.start()

    factor = 1.0 / math.sqrt(size)
    for m in range(slots):
        pl.when(first)(copies[m].wait)
        flat = u_ref.at[m].reshape(u_ref.shape[1] * u_ref.shape[2], LANES)
        total = jnp.zeros((8, tile), jnp.float32)
        for i in range(count):
            panels = []
            for at, pair in enumerate(pairs):
                if pair[0] == i:
                    for half in range(halves):
                        panels.append(flat[pl.ds((at * halves + half) * BLOCK, BLOCK), :])
            strip = jnp.concatenate(panels, axis=1)
            image = jnp.dot(strip, c_ref[pl.ds(i * BLOCK, size - i * BLOCK), :], preferred_element_type=jnp.float32)
            term = image * c_ref[pl.ds(i * BLOCK, BLOCK), :].astype(jnp.float32)
            total = total + jnp.sum(term.reshape(BLOCK // 8, 8, tile), axis=0)
        out_ref[pl.ds(m, 1), :] = jnp.sum(total, axis=0, keepdims=True) * factor


def quadratic(gathered, coeffs, tile=512):
    size, width = coeffs.shape
    parts, slots, rows, lanes = gathered.shape
    return pl.pallas_call(
        quadratic_kernel,
        grid=(width // tile,),
        out_shape=jax.ShapeDtypeStruct((slots, width), jnp.float32),
        in_specs=[
            pl.BlockSpec(memory_space=pl.ANY),
            pl.BlockSpec((size, tile), lambda i: (0, i)),
        ],
        out_specs=pl.BlockSpec((slots, tile), lambda i: (0, i)),
        scratch_shapes=[
            pltpu.VMEM((slots, parts, rows, lanes), jnp.bfloat16),
            pltpu.SemaphoreType.DMA((slots,)),
        ],
        compiler_params=pltpu.CompilerParams(vmem_limit_bytes=40 << 20),
        cost_estimate=pl.CostEstimate(
            flops=2 * slots * parts * rows * lanes * width, bytes_accessed=6 * size * width, transcendentals=0
        ),
        name="quadratic",
    )(gathered, coeffs)


def local(parts, density, flags, courant, spectral, tensor, owner):
    folded = fold(tensor)
    pieces = lax.all_to_all(folded.reshape(parts, -1, LANES), "dev", split_axis=0, concat_axis=0, tiled=True)
    chosen = jnp.stack([lax.dynamic_index_in_dim(pieces, owner[m], 0, keepdims=False) for m in range(owner.shape[0])])
    gathered = lax.all_gather(chosen, "dev", axis=0)
    moved = advect(density, flags, courant, parts)
    arrived = lax.all_to_all(moved, "dev", split_axis=0, concat_axis=0, tiled=True)
    coeffs = transform(spectral, arrived.reshape(-1, arrived.shape[2]))
    return (coeffs, quadratic(gathered, coeffs))


def solution(mesh):
    in_specs = (P("dev", None), P("dev"), P("dev"), P(), P("dev", None, None), P())
    out_specs = (P(None, "dev"), P(None, "dev"))

    def step(*args):
        return local(mesh.shape["dev"], *args)

    return jax.shard_map(step, mesh=mesh, in_specs=in_specs, out_specs=out_specs, check_vma=False)
```

time: 261 us -> 177 us (0.68)
  waiting for transfers between devices: 182 us -> 48.2 us
  blocking collectives: 0 us -> 57.5 us
  matrix products: 31.3 us -> 0 us
  Pallas kernels: 0 us -> 27.5 us
  other arithmetic: 12.9 us -> 0.63 us
  between operations: 16.7 us -> 21.7 us
  local copies, waits for them, and re-layouts: 5.82 us -> 9.12 us
    psum x1 -> x0, waiting for transfers between devices: 134 us -> none  [spread(): return lax.psum(jnp.where(mine, x, jnp.zeros_like(x)), axis)]
    all_to_all x0 -> x1, blocking collectives: none -> 57.5 us  [local(): lax.all_to_all(moved, 'dev', split_axis=0, concat_axis=0, tiled=True)]
    all_to_all x1, waiting for transfers between devices: 48.6 us -> 13.8 us  [local(): lax.all_to_all(folded.reshape(parts, -1, LANES), 'dev', split_axis=0, con...]
    all_gather x0 -> x1, waiting for transfers between devices: none -> 34.4 us  [local(): gathered = lax.all_gather(chosen, 'dev', axis=0)]
    dot_general x5 -> x0, matrix products: 31.3 us -> none  [the longest x4 22.9 us: quadratic(): image = jnp.dot(slab, coeffs, preferred_element_type=jnp.float32)]
    pallas_call x0 -> x4, Pallas kernels: none -> 27.5 us  [the longest x1 15.2 us: quadratic(): pl.pallas_call(quadratic_kernel, grid=(width // tile,), out_shape=jax.Sha...]
    unnamed x18 -> x16, local copies, waits for them, and re-layouts: 0.04 us -> 8.46 us
    convert_element_type x1 -> x0, other arithmetic: 7.23 us -> none  [upwind_step(): return (field - rate * (field - neighbour)).astype(jnp.bfloat16)]
  transfers between devices with their start and end apart: 2 -> 2, of which waited for: 2 -> 2; matrix products, arithmetic and copies ran while one was open for 5% -> 0% of each run, Pallas kernels for 0% -> 6%
where the time goes in v1:
time: 177 us; the launch traced here: 176 us
  blocking collectives  57.5 us (32%)
  waiting for transfers between devices  48.2 us (27%)
  Pallas kernels  27.5 us (16%)
  between operations  21.7 us (12%)
  starting transfers between devices  11.5 us (6%)
  local copies, waits for them, and re-layouts  9.12 us (5%)
    all_to_all x1, blocking collectives, local(): lax.all_to_all(moved, 'dev', split_axis=0, concat_axis=0, tiled=True)  57.5 us
    all_gather x1, waiting for transfers between devices, local(): gathered = lax.all_gather(chosen, 'dev', axis=0)  34.4 us
    pallas_call x1, Pallas kernels, quadratic(): pl.pallas_call(quadratic_kernel, grid=(width // tile,), out_shape=jax.Sha...  15.2 us
    all_to_all x1, waiting for transfers between devices, local(): lax.all_to_all(folded.reshape(parts, -1, LANES), 'dev', split_axis=0, con...  13.8 us
    all_to_all x1, starting transfers between devices, local(): lax.all_to_all(folded.reshape(parts, -1, LANES), 'dev', split_axis=0, con...  11.5 us
    unnamed x16, local copies, waits for them, and re-layouts  8.46 us
    pallas_call x1, Pallas kernels, transform(): pl.pallas_call(transform_kernel, grid=(width // tile,), out_shape=jax.Sha...  6.33 us
    pallas_call x1, Pallas kernels, advect(): pl.pallas_call(advect_kernel, grid=(parts // GROUP,), out_shape=jax.Shape...  4.59 us
  transfers between devices with their start and end apart: 2, of which 2 were waited for; matrix products, arithmetic and copies ran while one was open for 0% of the time, Pallas kernels for 6%

profile of v1, /device:TPU:1, one launch (start us, length us, event | category | flops | bytes accessed | tf_op | source)
XLA Modules:
  0.0 176.2 jit_solution(10165112938348746559)
XLA Ops:
  7.2 0.0 copy-start.1
  7.2 1.6 copy-done.1
  8.8 0.0 copy-start.7
  8.8 0.0 copy-start.2
  8.8 0.0 copy-start.3
  8.8 1.4 fold.1
  10.2 11.5 %all-to-all-start.1 = ((bf16[128,40,128]{2,1,0:T(8,128)(2,1)}), bf16[128,40,128]{2,1,0:T(8,128)(2,1)S(1)}, u32[]{:S(2)}, u32[]{:S(2)}) async-start(bf16[128,40,128]{2,1,0:T(8,128)(2,1)} %bitcast.1), calls=%async_computation.1 | async-start | bytes 2621440 | tf_op jit(solution)/shard_map/all_to_all | solution.py:172
  21.7 0.0 all-gather.3.cloned.1.call-start
  21.7 0.0 copy-done.7
  21.7 0.7 fusion
  30.0 13.8 %all-to-all-done.1 = bf16[128,40,128]{2,1,0:T(8,128)(2,1)S(1)} async-done(((bf16[128,40,128]{2,1,0:T(8,128)(2,1)}), bf16[128,40,128]{2,1,0:T(8,128)(2,1)S(1)}, u32[]{:S(2)}, u32[]{:S(2)}) %all-to-all-start.1) | async-done | bytes 1310752 | tf_op jit(solution)/shard_map/all_to_all | solution.py:172
  43.8 0.6 pad_maximum_fusion
  44.4 0.0 all-gather.3.cloned.1.call-update
  44.4 0.0 copy-done.2
  44.4 0.0 copy-done.3
  44.4 0.0 copy-start
  44.4 2.2 %copy-done = bf16[8,262144]{1,0:T(8,128)(2,1)S(1)} copy-done((bf16[8,262144]{1,0:T(8,128)(2,1)S(1)}, bf16[8,262144]{1,0:T(8,128)(2,1)}, u32[]{:S(2)}) %copy-start) | copy-done | bytes 4194328
  46.6 4.6 %advect.1 = bf16[128,8,2048]{2,1,0:T(8,128)(2,1)S(1)} custom-call(s32[8]{0:T(128)S(1)} %copy-done.2, f32[8]{0:T(128)S(1)} %copy-done.3, bf16[8,262144]{1,0:T(8,128)(2,1)S(1)} %copy-done, bf16[8,262144]{1,0:T(8,128)(2,1)S(1)} %copy-done, bf16[8,262144]{1,0:T(8,128)(2,1)S(1)} %copy-done), custom_call_target="tpu_custom_call" | custom-call | flops 8388608 | bytes 8388608 | tf_op jit(solution)/shard_map/advect/pallas_call | solution.py:73
  51.2 0.0 copy-start.5
  51.2 57.5 %all_to_all.10 = bf16[128,8,2048]{2,1,0:T(8,128)(2,1)S(1)} all-to-all(bf16[128,8,2048]{2,1,0:T(8,128)(2,1)S(1)} %advect.1), channel_id=1, replica_groups=mesh['dev'=128] {'dev'}, dimensions={0} | all-to-all | bytes 8388608 | tf_op jit(solution)/shard_map/all_to_all | solution.py:176
  108.8 0.0 copy-done.5
  108.8 6.3 %transform.1.c_ref = bf16[1024,2048]{1,0:T(8,128)(2,1)} custom-call(bf16[1024,1024]{1,0:T(8,128)(2,1)S(1)} %copy-done.5, bf16[1024,2048]{1,0:T(8,128)(2,1)S(1)} %bitcast.7), custom_call_target="tpu_custom_call" | custom-call | flops 4294967296 | bytes 12582912 | tf_op jit(solution)/shard_map/transform/pallas_call | solution.py:97
  115.1 34.4 %all-gather.3.cloned.1.call-done = bf16[512,40,128]{2,1,0:T(8,128)(2,1)} async-done(((bf16[4,40,128]{2,1,0:T(8,128)(2,1)}), bf16[512,40,128]{2,1,0:T(8,128)(2,1)}) %all-gather.3.cloned.1.call-update) | async-done | bytes 5242896 | tf_op jit(solution)/shard_map/all_gather | solution.py:174
  149.5 0.0 copy-start.4
  149.5 2.5 %copy-done.4 = bf16[512,40,128]{2,1,0:T(8,128)(2,1)S(1)} copy-done((bf16[512,40,128]{2,1,0:T(8,128)(2,1)S(1)}, bf16[512,40,128]{2,1,0:T(8,128)(2,1)}, u32[]{:S(2)}) %copy-start.4) | copy-done | bytes 5242904
  151.9 0.0 copy-start.6
  152.0 2.2 %copy-done.6 = bf16[1024,2048]{1,0:T(8,128)(2,1)S(1)} copy-done((bf16[1024,2048]{1,0:T(8,128)(2,1)S(1)}, bf16[1024,2048]{1,0:T(8,128)(2,1)}, u32[]{:S(2)}) %copy-start.6) | copy-done | bytes 4194328
  154.1 15.2 %quadratic.1 = f32[4,2048]{1,0:T(4,128)} custom-call(bf16[128,4,40,128]{3,2,1,0:T(8,128)(2,1)S(1)} %bitcast.8, bf16[1024,2048]{1,0:T(8,128)(2,1)S(1)} %copy-done.6), custom_call_target="tpu_custom_call" | custom-call | flops 10737418240 | bytes 12582912 | tf_op jit(solution)/shard_map/quadratic/pallas_call | solution.py:149
  (1 shorter events, 0.0 us)
Async XLA Ops:
  7.2 1.6 copy-start.1
  8.8 13.0 %copy-start.7 = (s32[4]{0:T(128)S(1)}, s32[4]{0:T(128)}, u32[]{:S(2)}) copy-start(s32[4]{0:T(128)} %param.11) | copy-start | bytes 52
  8.8 35.7 %copy-start.2 = (s32[8]{0:T(128)S(1)}, s32[8]{0:T(128)}, u32[]{:S(2)}) copy-start(s32[8]{0:T(128)} %flags_ref.1) | copy-start | bytes 100
  8.8 35.7 %copy-start.3 = (f32[8]{0:T(128)S(1)}, f32[8]{0:T(128)}, u32[]{:S(2)}) copy-start(f32[8]{0:T(128)} %courant_ref.1) | copy-start | bytes 100
  10.2 33.6 %all-to-all-start.1 = ((bf16[128,40,128]{2,1,0:T(8,128)(2,1)}), bf16[128,40,128]{2,1,0:T(8,128)(2,1)S(1)}, u32[]{:S(2)}, u32[]{:S(2)}) async-start(bf16[128,40,128]{2,1,0:T(8,128)(2,1)} %bitcast.1), calls=%async_computation.1 | async-start | bytes 2621440 | tf_op jit(solution)/shard_map/all_to_all | solution.py:172
  21.7 127.8 %all-gather.3.cloned.1.call-start = ((), (), s32[]{:S(2)}) async-start(), calls=%async_computation.2 | async-start | bytes 5283840 | tf_op jit(solution)/shard_map/all_gather | solution.py:174
  44.4 2.2 %copy-start = (bf16[8,262144]{1,0:T(8,128)(2,1)S(1)}, bf16[8,262144]{1,0:T(8,128)(2,1)}, u32[]{:S(2)}) copy-start(bf16[8,262144]{1,0:T(8,128)(2,1)} %after_ref.1) | copy-start | bytes 12582916
  51.2 57.5 %copy-start.5 = (bf16[1024,1024]{1,0:T(8,128)(2,1)S(1)}, bf16[1024,1024]{1,0:T(8,128)(2,1)}, u32[]{:S(2)}) copy-start(bf16[1024,1024]{1,0:T(8,128)(2,1)} %s_ref.1) | copy-start | bytes 6291460
  149.5 2.5 %copy-start.4 = (bf16[512,40,128]{2,1,0:T(8,128)(2,1)S(1)}, bf16[512,40,128]{2,1,0:T(8,128)(2,1)}, u32[]{:S(2)}) copy-start(bf16[512,40,128]{2,1,0:T(8,128)(2,1)} %all-gather.3.cloned.1.call-done) | copy-start | bytes 15728644
  151.9 2.2 %copy-start.6 = (bf16[1024,2048]{1,0:T(8,128)(2,1)S(1)}, bf16[1024,2048]{1,0:T(8,128)(2,1)}, u32[]{:S(2)}) copy-start(bf16[1024,2048]{1,0:T(8,128)(2,1)} %transform.1.c_ref) | copy-start | bytes 12582916
Sparse Core Ops, SparseCore 0:
  44.5 104.8 all-gather.2

commit v2 on v1

v2 whole, which is shorter than its diff:
```python
import functools
import math

import jax
import jax.numpy as jnp
from jax import lax
from jax.experimental import pallas as pl
from jax.experimental.pallas import tpu as pltpu
from jax.sharding import PartitionSpec as P

BLOCK = 256
LANES = 128
GROUP = 8
SUBLANES = 8
LIMIT = 60 << 20


def fold_kernel(t_hbm, u_ref, e_ref, t_ref, sems):
    count = t_ref.shape[0] // BLOCK
    halves = BLOCK // LANES
    copies = []
    for i in range(count):
        rows = pl.ds(i * BLOCK, BLOCK)
        copies.append(pltpu.make_async_copy(t_hbm.at[0, rows, :], t_ref.at[rows, :], sems.at[i]))
        copies[i].start()

    def load(i, j):
        return t_ref[pl.ds(i * BLOCK, BLOCK), pl.ds(j * BLOCK, BLOCK)].astype(jnp.float32)

    def store(at, block):
        block = block.astype(jnp.bfloat16)
        for half in range(halves):
            u_ref[pl.ds((at * halves + half) * BLOCK, BLOCK), :] = block[:, half * LANES : (half + 1) * LANES]

    row = lax.broadcasted_iota(jnp.int32, (BLOCK, BLOCK), 0)
    col = lax.broadcasted_iota(jnp.int32, (BLOCK, BLOCK), 1)
    above = above_pairs(count)
    e_ref[...] = jnp.zeros_like(e_ref)
    for j in range(count):
        copies[j].wait()
        for i in range(j):
            store(above.index((i, j)), load(i, j) + load(j, i).T)
        if j % 2 == 1:
            upper, lower = load(j - 1, j - 1), load(j, j)
            packed = jnp.where(row < col, upper + upper.T, jnp.where(row == col, upper, lower + lower.T))
            store(len(above) + j // 2, packed)
            line = jnp.sum(jnp.where(row == col, lower, 0.0), axis=0, keepdims=True).astype(jnp.bfloat16)
            for half in range(halves):
                e_ref[pl.ds(j // 2 * halves + half, 1), :] = line[:, half * LANES : (half + 1) * LANES]


def above_pairs(count):
    return [(i, j) for j in range(count) for i in range(j)]


def fold(tensor):
    size = tensor.shape[1]
    count = size // BLOCK
    rows = (len(above_pairs(count)) + count // 2) * BLOCK * (BLOCK // LANES)
    return pl.pallas_call(
        fold_kernel,
        out_shape=[
            jax.ShapeDtypeStruct((rows, LANES), jnp.bfloat16),
            jax.ShapeDtypeStruct((SUBLANES, LANES), jnp.bfloat16),
        ],
        in_specs=[pl.BlockSpec(memory_space=pltpu.HBM)],
        out_specs=[pl.BlockSpec(memory_space=pltpu.VMEM)] * 2,
        scratch_shapes=[pltpu.VMEM((size, size), jnp.bfloat16), pltpu.SemaphoreType.DMA((count,))],
        compiler_params=pltpu.CompilerParams(vmem_limit_bytes=LIMIT),
        cost_estimate=pl.CostEstimate(flops=2 * size * size, bytes_accessed=3 * size * size, transcendentals=0),
        name="fold",
    )(tensor)


def advect_kernel(flags_ref, courant_ref, before_ref, here_ref, after_ref, out_ref):
    nodes = here_ref.shape[0]
    width = here_ref.shape[1] // out_ref.shape[0]
    row = lax.broadcasted_iota(jnp.int32, (nodes, 1), 0)
    flag = jnp.zeros((nodes, 1), jnp.int32)
    rate = jnp.zeros((nodes, 1), jnp.float32)
    for r in range(nodes):
        flag = jnp.where(row == r, flags_ref[r], flag)
        rate = jnp.where(row == r, courant_ref[r], rate)
    upward = jnp.broadcast_to(flag, (nodes, width)) == 1
    for d in range(out_ref.shape[0]):
        start, stop = d * width, (d + 1) * width
        last = d == out_ref.shape[0] - 1
        before = before_ref[...] if d == 0 else here_ref[:, start - LANES : start]
        after = after_ref[...] if last else here_ref[:, stop : stop + LANES]
        field = here_ref[:, start:stop].astype(jnp.float32)
        line = jnp.concatenate([before.astype(jnp.float32), field, after.astype(jnp.float32)], axis=1)
        left = pltpu.roll(line, 1, axis=1)[:, LANES : LANES + width]
        right = pltpu.roll(line, width + 2 * LANES - 1, axis=1)[:, LANES : LANES + width]
        neighbour = jnp.where(upward, left, right)
        moved = (field - rate * (field - neighbour)).astype(jnp.bfloat16)
        for t in range(width // LANES):
            out_ref[d, t * nodes : (t + 1) * nodes, :] = moved[:, t * LANES : (t + 1) * LANES]


def advect(density, flags, courant, parts, spare):
    nodes, cells = density.shape
    width = cells // parts
    wide = GROUP * width // LANES
    lines = cells // LANES
    rows = nodes * width // LANES
    return pl.pallas_call(
        advect_kernel,
        grid=(parts // GROUP,),
        out_shape=jax.ShapeDtypeStruct((parts, rows + spare, LANES), jnp.bfloat16),
        in_specs=[
            pl.BlockSpec(memory_space=pltpu.SMEM),
            pl.BlockSpec(memory_space=pltpu.SMEM),
            pl.BlockSpec((nodes, LANES), lambda i: (0, (i * wide + lines - 1) % lines)),
            pl.BlockSpec((nodes, GROUP * width), lambda i: (0, i)),
            pl.BlockSpec((nodes, LANES), lambda i: (0, ((i + 1) * wide) % lines)),
        ],
        out_specs=pl.BlockSpec((GROUP, rows, LANES), lambda i: (i, 0, 0)),
        compiler_params=pltpu.CompilerParams(vmem_limit_bytes=LIMIT),
        cost_estimate=pl.CostEstimate(flops=4 * nodes * cells, bytes_accessed=4 * nodes * cells, transcendentals=0),
        name="advect",
    )(flags, courant, density, density, density)


def pick_kernel(owner_ref, pieces_ref, extra_ref, _, out_hbm, spread_ref, sems):
    half = owner_ref.shape[0] // 2
    batch, rows = spread_ref.shape[0], spread_ref.shape[1]
    first = out_hbm.shape[1] - rows
    chosen = [pieces_ref[owner_ref[m]] for m in range(2 * half)]
    extra = extra_ref[...]
    for d in range(batch):
        core, z, y = d % 2, d // 2 % 4, d // 8 % 4
        quarter = (y if core else z) * SUBLANES
        for s in range(half):
            part = chosen[core * half + s][quarter : quarter + SUBLANES, :]
            spread_ref[d, s * SUBLANES : (s + 1) * SUBLANES, :] = part
        spread_ref[d, half * SUBLANES : (half + 1) * SUBLANES, :] = extra
    writes = []
    for b in range(out_hbm.shape[0] // batch):
        target = out_hbm.at[pl.ds(b * batch, batch), pl.ds(first, rows), :]
        writes.append(pltpu.make_async_copy(spread_ref, target, sems.at[b]))
    for write in writes:
        write.start()
    for write in writes:
        write.wait()


def pick(owner, pieces, extra, moved, spare, batch=32):
    parts = pieces.shape[0]
    return pl.pallas_call(
        pick_kernel,
        out_shape=jax.ShapeDtypeStruct(moved.shape, moved.dtype),
        in_specs=[
            pl.BlockSpec(memory_space=pltpu.SMEM),
            pl.BlockSpec(memory_space=pltpu.VMEM),
            pl.BlockSpec(memory_space=pltpu.VMEM),
            pl.BlockSpec(memory_space=pltpu.HBM),
        ],
        out_specs=pl.BlockSpec(memory_space=pltpu.HBM),
        scratch_shapes=[
            pltpu.VMEM((batch, spare, LANES), jnp.bfloat16),
            pltpu.SemaphoreType.DMA((parts // batch,)),
        ],
        input_output_aliases={3: 0},
        compiler_params=pltpu.CompilerParams(vmem_limit_bytes=32 << 20),
        cost_estimate=pl.CostEstimate(flops=0, bytes_accessed=parts * spare * LANES * 2, transcendentals=0),
        name="pick",
    )(owner, pieces, extra, moved)


def unpack_kernel(owner_ref, arrived, near_ref, e_ref, sems):
    slots = e_ref.shape[0]
    end = arrived.shape[1] - SUBLANES
    first = end - near_ref.shape[1]
    copies = [pltpu.make_async_copy(arrived.at[:, pl.ds(first, end - first), :], near_ref, sems.at[slots])]
    for m in range(slots):
        last = arrived.at[owner_ref[m], pl.ds(end, SUBLANES), :]
        copies.append(pltpu.make_async_copy(last, e_ref.at[m], sems.at[m]))
    for copy in copies:
        copy.start()
    for copy in copies:
        copy.wait()


def unpack(owner, arrived, rows):
    slots = owner.shape[0]
    parts = arrived.shape[0]
    return pl.pallas_call(
        unpack_kernel,
        out_shape=[
            jax.ShapeDtypeStruct((parts, rows, LANES), jnp.bfloat16),
            jax.ShapeDtypeStruct((slots, SUBLANES, LANES), jnp.bfloat16),
        ],
        in_specs=[pl.BlockSpec(memory_space=pltpu.SMEM), pl.BlockSpec(memory_space=pl.ANY)],
        out_specs=[pl.BlockSpec(memory_space=pltpu.VMEM)] * 2,
        scratch_shapes=[pltpu.SemaphoreType.DMA((slots + 1,))],
        compiler_params=pltpu.CompilerParams(vmem_limit_bytes=LIMIT),
        cost_estimate=pl.CostEstimate(flops=0, bytes_accessed=4 * parts * rows * LANES, transcendentals=0),
        name="unpack",
    )(owner, arrived)


def transform_kernel(s_ref, x_ref, c_ref):
    parts, rows, lanes = x_ref.shape
    nodes = s_ref.shape[1] // parts
    columns = [x_ref[:, t : t + nodes, :].reshape(parts * nodes, lanes) for t in range(0, rows, nodes)]
    block = jnp.concatenate(columns, axis=1)
    c_ref[...] = jnp.dot(s_ref[...], block, preferred_element_type=jnp.float32).astype(jnp.bfloat16)


def transform(spectral, arrived, width, tile=512):
    size = spectral.shape[0]
    parts = arrived.shape[0]
    nodes = spectral.shape[1] // parts
    return pl.pallas_call(
        transform_kernel,
        grid=(width // tile,),
        out_shape=jax.ShapeDtypeStruct((size, width), jnp.bfloat16),
        in_specs=[
            pl.BlockSpec(spectral.shape, lambda i: (0, 0)),
            pl.BlockSpec((parts, nodes * tile // LANES, LANES), lambda i: (0, i, 0)),
        ],
        out_specs=pl.BlockSpec((size, tile), lambda i: (0, i)),
        compiler_params=pltpu.CompilerParams(vmem_limit_bytes=LIMIT),
        cost_estimate=pl.CostEstimate(
            flops=2 * size * size * width, bytes_accessed=6 * size * width, transcendentals=0
        ),
        name="transform",
    )(spectral, arrived)


def quadratic_kernel(mine, q0, q1, q2, q3, e_ref, c_ref, *refs):
    before_ref = None if mine else refs[0]
    out_ref, u_ref, sems = refs[-3:]
    size, tile = c_ref.shape
    count = size // BLOCK
    half = u_ref.shape[0]
    halves = BLOCK // LANES
    above = above_pairs(count)
    first = pl.program_id(0) == 0
    here = lax.axis_index("dev")
    core = here % 2 if mine else 1 - here % 2
    start = jnp.where(core == 0, here // 2, here // 8)
    copies = []
    for s in range(half):
        for k, source in enumerate((q0, q1, q2, q3)):
            quarter = (start + 4 - k) % 4
            rows = source.at[:, pl.ds(s * SUBLANES, SUBLANES), :]
            copies.append(pltpu.make_async_copy(rows, u_ref.at[s, :, quarter], sems.at[s, k]))

    def panel(flat, at):
        parts = [flat[pl.ds((at * halves + part) * BLOCK, BLOCK), :] for part in range(halves)]
        return jnp.concatenate(parts, axis=1)

    @pl.when(first)
    def _():
        for copy in copies:
            copy.start()

    if not mine:
        out_ref[...] = before_ref[...]
    factor = 1.0 / math.sqrt(size)
    row = lax.broadcasted_iota(jnp.int32, (BLOCK, BLOCK), 0)
    col = lax.broadcasted_iota(jnp.int32, (BLOCK, BLOCK), 1)
    for s in range(half):

        @pl.when(first)
        def _():
            for copy in copies[s * 4 : s * 4 + 4]:
                copy.wait()

        flat = u_ref.at[s].reshape(math.prod(u_ref.shape[1:4]), LANES)
        total = jnp.zeros((SUBLANES, tile), jnp.float32)
        for i in range(count):
            packed = panel(flat, len(above) + i // 2).astype(jnp.float32)
            if i % 2 == 0:
                diagonal = jnp.where(row <= col, packed, 0.0)
            else:
                lines = [e_ref[core * half + s, pl.ds(i // 2 * halves + part, 1), :] for part in range(halves)]
                line = jnp.concatenate(lines, axis=1).astype(jnp.float32)
                diagonal = jnp.where(row > col, packed, jnp.where(row == col, line, 0.0))
            panels = [diagonal.astype(jnp.bfloat16)]
            panels += [panel(flat, above.index((i, j))) for j in range(i + 1, count)]
            strip = jnp.concatenate(panels, axis=1)
            image = jnp.dot(strip, c_ref[pl.ds(i * BLOCK, size - i * BLOCK), :], preferred_element_type=jnp.float32)
            term = image * c_ref[pl.ds(i * BLOCK, BLOCK), :].astype(jnp.float32)
            total = total + jnp.sum(term.reshape(BLOCK // SUBLANES, SUBLANES, tile), axis=0)
        out_ref[pl.ds(core * half + s, 1), :] = jnp.sum(total, axis=0, keepdims=True) * factor


def quadratic(quarters, diagonals, coeffs, before, tile=512):
    size, width = coeffs.shape
    parts = quarters[0].shape[0]
    slots = diagonals.shape[0]
    half = slots // 2
    out_spec = pl.BlockSpec((slots, tile), lambda i: (0, i))
    args = [*quarters, diagonals, coeffs]
    in_specs = [
        *[pl.BlockSpec(memory_space=pl.ANY)] * 4,
        pl.BlockSpec(diagonals.shape, lambda i: (0, 0, 0)),
        pl.BlockSpec((size, tile), lambda i: (0, i)),
    ]
    if before is not None:
        args.append(before)
        in_specs.append(out_spec)
    return pl.pallas_call(
        functools.partial(quadratic_kernel, before is None),
        grid=(width // tile,),
        out_shape=jax.ShapeDtypeStruct((slots, width), jnp.float32),
        in_specs=in_specs,
        out_specs=out_spec,
        scratch_shapes=[
            pltpu.VMEM((half, parts, 4, SUBLANES, LANES), jnp.bfloat16),
            pltpu.SemaphoreType.DMA((half, 4)),
        ],
        compiler_params=pltpu.CompilerParams(vmem_limit_bytes=48 << 20),
        cost_estimate=pl.CostEstimate(
            flops=half * size * size * width * 5 // 4, bytes_accessed=2 * size * width, transcendentals=0
        ),
        name="quadratic",
    )(*args)


def exchange(x):
    return lax.all_to_all(x, "dev", split_axis=0, concat_axis=0, tiled=True)


def shift(parts, k):
    pairs = []
    for d in range(parts):
        step = 8 if d % 2 else 2
        at = d // step % 4
        pairs.append((d, d + ((at + k) % 4 - at) * step))
    return pairs


def local(parts, density, flags, courant, spectral, tensor, owner):
    half = owner.shape[0] // 2
    width = density.shape[1] // parts
    spare = (half + 1) * SUBLANES
    folded, extra = fold(tensor)
    pieces = exchange(folded.reshape(parts, -1, LANES))
    moved = advect(density, flags, courant, parts, spare)
    arrived = exchange(pick(owner, pieces, extra, moved, spare))
    first, diagonals = unpack(owner, arrived, half * SUBLANES)
    near = [first] + [lax.ppermute(first, "dev", shift(parts, k)) for k in (1, 2, 3)]
    coeffs = transform(spectral, arrived, width)
    *near, coeffs = lax.optimization_barrier((*near, coeffs))
    far = [lax.ppermute(x, "dev", [(d, d ^ 1) for d in range(parts)]) for x in near]
    own = quadratic(near, diagonals, coeffs, None)
    return (coeffs, quadratic(far, diagonals, coeffs, own))


def solution(mesh):
    in_specs = (P("dev", None), P("dev"), P("dev"), P(), P("dev", None, None), P())
    out_specs = (P(None, "dev"), P(None, "dev"))

    def step(*args):
        return local(mesh.shape["dev"], *args)

    return jax.shard_map(step, mesh=mesh, in_specs=in_specs, out_specs=out_specs, check_vma=False)
```

time: 177 us -> 144 us (0.81)
  waiting for transfers between devices: 48.2 us -> 13.7 us
  between operations: 21.7 us -> 0.74 us
  Pallas kernels: 27.5 us -> 44.3 us
  blocking collectives: 57.5 us -> 66.2 us
  local copies, waits for them, and re-layouts: 9.12 us -> 2.44 us
  starting transfers between devices: 11.5 us -> 16.1 us
    all_gather x1 -> x0, waiting for transfers between devices: 34.4 us -> none  [local(): gathered = lax.all_gather(chosen, 'dev', axis=0)]
    all_to_all x1, blocking collectives: 57.5 us -> 66.2 us  [exchange(): return lax.all_to_all(x, 'dev', split_axis=0, concat_axis=0, tiled=True)]
    pallas_call x2 -> x5, Pallas kernels: 16.6 us -> 24.1 us  [the longest x2 18.1 us: quadratic(): pl.pallas_call(functools.partial(quadratic_kernel, before is None), grid=...]
    pallas_call x1, Pallas kernels: 4.59 us -> 11.8 us  [advect(): pl.pallas_call(advect_kernel, grid=(parts // GROUP,), out_shape=jax.Shape...]
    all_to_all x1, waiting for transfers between devices: 13.8 us -> 7.46 us  [exchange(): return lax.all_to_all(x, 'dev', split_axis=0, concat_axis=0, tiled=True)]
    ppermute x0 -> x7, waiting for transfers between devices: none -> 6.2 us  [the longest x3 6.19 us: local(): lax.ppermute(first, 'dev', shift(parts, k))]
    unnamed x16 -> x10, local copies, waits for them, and re-layouts: 8.46 us -> 2.44 us
    ppermute x0 -> x7, starting transfers between devices: none -> 4.56 us  [the longest x4 2.48 us: local(): lax.ppermute(x, 'dev', [(d, d ^ 1) for d in range(parts)])]
  transfers between devices with their start and end apart: 2 -> 8, of which waited for: 2 -> 3; matrix products, arithmetic and copies ran while one was open for 0% -> 0% of each run, Pallas kernels for 6% -> 20%
where the time goes in v2:
time: 144 us; the launch traced here: 143 us
  blocking collectives  66.2 us (46%)
  Pallas kernels  44.3 us (31%)
  starting transfers between devices  16.1 us (11%)
  waiting for transfers between devices  13.7 us (10%)
  local copies, waits for them, and re-layouts  2.44 us (2%)
    all_to_all x1, blocking collectives, exchange(): return lax.all_to_all(x, 'dev', split_axis=0, concat_axis=0, tiled=True)  66.2 us
    pallas_call x2, Pallas kernels, quadratic(): pl.pallas_call(functools.partial(quadratic_kernel, before is None), grid=...  18.1 us
    pallas_call x1, Pallas kernels, advect(): pl.pallas_call(advect_kernel, grid=(parts // GROUP,), out_shape=jax.Shape...  11.8 us
    all_to_all x1, starting transfers between devices, exchange(): return lax.all_to_all(x, 'dev', split_axis=0, concat_axis=0, tiled=True)  11.5 us
    pallas_call x1, Pallas kernels, transform(): pl.pallas_call(transform_kernel, grid=(width // tile,), out_shape=jax.Sha...  8.38 us
    all_to_all x1, waiting for transfers between devices, exchange(): return lax.all_to_all(x, 'dev', split_axis=0, concat_axis=0, tiled=True)  7.46 us
    ppermute x3, waiting for transfers between devices, local(): lax.ppermute(first, 'dev', shift(parts, k))  6.19 us
  transfers between devices with their start and end apart: 8, of which 3 were waited for; matrix products, arithmetic and copies ran while one was open for 0% of the time, Pallas kernels for 20%

profile of v2, /device:TPU:1, one launch (start us, length us, event | category | flops | bytes accessed | tf_op | source)
XLA Modules:
  0.0 143.4 jit_solution(2162895260768793809)
XLA Ops:
  0.6 2.8 %fold.1 = (bf16[4096,128]{1,0:T(8,128)(2,1)}, bf16[8,128]{1,0:T(8,128)(2,1)}) custom-call(bf16[1,1024,1024]{2,1,0:T(8,128)(2,1)} %t_hbm.1), custom_call_target="tpu_custom_call" | custom-call | flops 2097152 | bytes 3145728 | tf_op jit(solution)/shard_map/fold/pallas_call | solution.py:60
  3.4 11.5 %all-to-all-start = ((bf16[128,32,128]{2,1,0:T(8,128)(2,1)}), bf16[128,32,128]{2,1,0:T(8,128)(2,1)S(1)}, u32[]{:S(2)}, u32[]{:S(2)}) async-start(bf16[128,32,128]{2,1,0:T(8,128)(2,1)} %bitcast.1), calls=%async_computation | async-start | bytes 2097152 | tf_op jit(solution)/shard_map/all_to_all | solution.py:324
  14.9 0.0 copy-start.1
  14.9 0.0 copy-start.2
  14.9 11.8 %advect.1._ = bf16[128,152,128]{2,1,0:T(8,128)(2,1)} custom-call(s32[8]{0:T(128)} %flags_ref.1, f32[8]{0:T(128)} %courant_ref.1, bf16[8,262144]{1,0:T(8,128)(2,1)} %after_ref.1, bf16[8,262144]{1,0:T(8,128)(2,1)} %after_ref.1, bf16[8,262144]{1,0:T(8,128)(2,1)} %after_ref.1), custom_call_target="tpu_custom_call" | custom-call | flops 8388608 | bytes 8388608 | tf_op jit(solution)/shard_map/advect/pallas_call | solution.py:106
  26.7 7.5 %all-to-all-done.pieces_ref = bf16[128,32,128]{2,1,0:T(8,128)(2,1)S(1)} async-done(((bf16[128,32,128]{2,1,0:T(8,128)(2,1)}), bf16[128,32,128]{2,1,0:T(8,128)(2,1)S(1)}, u32[]{:S(2)}, u32[]{:S(2)}) %all-to-all-start) | async-done | bytes 1048608 | tf_op jit(solution)/shard_map/all_to_all | solution.py:324
  34.2 0.0 copy-done.1
  34.2 0.0 copy-done.2
  34.2 2.4 %copy-done = bf16[128,152,128]{2,1,0:T(8,128)(2,1)S(1)} copy-done((bf16[128,152,128]{2,1,0:T(8,128)(2,1)S(1)}, bf16[128,152,128]{2,1,0:T(8,128)(2,1)}, u32[]{:S(2)}) %copy-start) | copy-done | bytes 4980760
  36.6 0.7 pick.1
  37.3 66.2 %all_to_all.10.arrived.x_ref = bf16[128,152,128]{2,1,0:T(8,128)(2,1)} all-to-all(bf16[128,152,128]{2,1,0:T(8,128)(2,1)S(1)} %pick.1), channel_id=1, replica_groups=mesh['dev'=128] {'dev'}, dimensions={0} | all-to-all | bytes 9961472 | tf_op jit(solution)/shard_map/all_to_all | solution.py:324
  103.5 2.6 %unpack.1 = (bf16[128,16,128]{2,1,0:T(8,128)(2,1)}, bf16[4,8,128]{2,1,0:T(8,128)(2,1)}) custom-call(s32[4]{0:T(128)} %owner_ref.3, bf16[128,152,128]{2,1,0:T(8,128)(2,1)} %all_to_all.10.arrived.x_ref), custom_call_target="tpu_custom_call" | custom-call | bytes 1048576 | tf_op jit(solution)/shard_map/unpack/pallas_call | solution.py:187
  106.1 0.0 copy-start.3
  106.1 0.0 copy-start.4
  106.1 1.0 collective-permute-start.2
  107.1 1.1 collective-permute-start.1
  108.2 0.0 collective-permute-start
  108.2 8.4 %transform.1.c_ref = bf16[1024,2048]{1,0:T(8,128)(2,1)} custom-call(bf16[1024,1024]{1,0:T(8,128)(2,1)} %s_ref.1, bf16[128,152,128]{2,1,0:T(8,128)(2,1)} %all_to_all.10.arrived.x_ref), custom_call_target="tpu_custom_call" | custom-call | flops 4294967296 | bytes 12582912 | tf_op jit(solution)/shard_map/transform/pallas_call | solution.py:214
  116.6 0.0 collective-permute-done.2.q3
  116.6 0.6 collective-permute-done.1.q2
  117.2 5.6 %collective-permute-done.q1 = bf16[128,16,128]{2,1,0:T(8,128)(2,1)S(1)} collective-permute-done((bf16[128,16,128]{2,1,0:T(8,128)(2,1)}, bf16[128,16,128]{2,1,0:T(8,128)(2,1)S(1)}, u32[]{:S(2)}, u32[]{:S(2)}) %collective-permute-start) | collective-permute-done | bytes 524320 | tf_op jit(solution)/shard_map/ppermute | solution.py:345
  122.8 0.0 copy-done.3
  122.8 2.0 %collective-permute-start.3 = (bf16[128,16,128]{2,1,0:T(8,128)(2,1)S(1)}, bf16[128,16,128]{2,1,0:T(8,128)(2,1)S(1)}, u32[]{:S(2)}, u32[]{:S(2)}) collective-permute-start(bf16[128,16,128]{2,1,0:T(8,128)(2,1)S(1)} %copy-done.3), channel_id=1, source_target_pairs={{0,1},{1,0},{2,3},{3,2},{4,5},{5,4},{6,7},{7,6},{8,9},{9,8},{10,11... | collective-permute-start | bytes 1572872 | tf_op jit(solution)/shard_map/ppermute | solution.py:348
  124.7 0.0 collective-permute-start.4
  124.7 0.5 collective-permute-start.5
  125.2 0.0 collective-permute-start.6
  125.2 8.7 %quadratic.2.refs_0_ = f32[4,2048]{1,0:T(4,128)S(1)} custom-call(bf16[128,16,128]{2,1,0:T(8,128)(2,1)S(1)} %copy-done.3, bf16[128,16,128]{2,1,0:T(8,128)(2,1)S(1)} %collective-permute-done.q1, bf16[128,16,128]{2,1,0:T(8,128)(2,1)S(1)} %collective-permute-done.1.q2, bf16[128,16,128]{2,1,0:T(8,128)(2,1)S(1)} %collective-permute-done.2.q3, ...), custom_call_target="tpu_custom_call" | custom-call | flops 5368709120 | bytes 4194304 | tf_op jit(solution)/shard_map/quadratic/pallas_call | solution.py:305
  134.0 0.0 collective-permute-done.3.q0
  134.0 0.0 collective-permute-done.4.q1
  134.0 0.0 collective-permute-done.5.q2
  134.0 0.0 collective-permute-done.6.q3
  134.0 9.4 %quadratic.3 = f32[4,2048]{1,0:T(4,128)} custom-call(bf16[128,16,128]{2,1,0:T(8,128)(2,1)S(1)} %collective-permute-done.3.q0, bf16[128,16,128]{2,1,0:T(8,128)(2,1)S(1)} %collective-permute-done.4.q1, bf16[128,16,128]{2,1,0:T(8,128)(2,1)S(1)} %collective-permute-done.5.q2, bf16[128,16,128]{2,1,0:T(8,128)(2,1)S(1)} %collective-permute-done.6.q3, ...), custom_call_target="tpu_custom_call" | custom-call | flops 5368709120 | bytes 4194304 | tf_op jit(solution)/shard_map/quadratic/pallas_call | solution.py:305
  (2 shorter events, 0.0 us)
Async XLA Ops:
  3.4 30.8 %all-to-all-start = ((bf16[128,32,128]{2,1,0:T(8,128)(2,1)}), bf16[128,32,128]{2,1,0:T(8,128)(2,1)S(1)}, u32[]{:S(2)}, u32[]{:S(2)}) async-start(bf16[128,32,128]{2,1,0:T(8,128)(2,1)} %bitcast.1), calls=%async_computation | async-start | bytes 2097152 | tf_op jit(solution)/shard_map/all_to_all | solution.py:324
  14.9 19.3 %copy-start.1 = (bf16[8,128]{1,0:T(8,128)(2,1)S(1)}, bf16[8,128]{1,0:T(8,128)(2,1)}, u32[]{:S(2)}) copy-start(bf16[8,128]{1,0:T(8,128)(2,1)} %get-tuple-element.12.extra_ref) | copy-start | bytes 6148
  14.9 19.3 %copy-start.2 = (s32[4]{0:T(128)S(1)}, s32[4]{0:T(128)}, u32[]{:S(2)}) copy-start(s32[4]{0:T(128)} %owner_ref.3) | copy-start | bytes 52
  34.2 2.4 %copy-start = (bf16[128,152,128]{2,1,0:T(8,128)(2,1)S(1)}, bf16[128,152,128]{2,1,0:T(8,128)(2,1)}, u32[]{:S(2)}) copy-start(bf16[128,152,128]{2,1,0:T(8,128)(2,1)} %advect.1._) | copy-start | bytes 14942212
  106.1 16.7 %copy-start.3 = (bf16[128,16,128]{2,1,0:T(8,128)(2,1)S(1)}, bf16[128,16,128]{2,1,0:T(8,128)(2,1)}, u32[]{:S(2)}) copy-start(bf16[128,16,128]{2,1,0:T(8,128)(2,1)} %get-tuple-element.15.q0) | copy-start | bytes 1572868
  106.1 19.1 %copy-start.4 = (bf16[4,8,128]{2,1,0:T(8,128)(2,1)S(1)}, bf16[4,8,128]{2,1,0:T(8,128)(2,1)}, u32[]{:S(2)}) copy-start(bf16[4,8,128]{2,1,0:T(8,128)(2,1)} %get-tuple-element.19.e_ref) | copy-start | bytes 24580
  106.1 10.5 %collective-permute-start.2 = (bf16[128,16,128]{2,1,0:T(8,128)(2,1)}, bf16[128,16,128]{2,1,0:T(8,128)(2,1)S(1)}, u32[]{:S(2)}, u32[]{:S(2)}) collective-permute-start(bf16[128,16,128]{2,1,0:T(8,128)(2,1)} %get-tuple-element.15.q0), channel_id=1, source_target_pairs={{0,6},{1,25},{2,0},{3,27},{4,2},{5,29},{6,4},{7,31},{8,14},{9,1},{... | collective-permute-start | bytes 1572872 | tf_op jit(solution)/shard_map/ppermute | solution.py:345
  107.1 10.1 %collective-permute-start.1 = (bf16[128,16,128]{2,1,0:T(8,128)(2,1)}, bf16[128,16,128]{2,1,0:T(8,128)(2,1)S(1)}, u32[]{:S(2)}, u32[]{:S(2)}) collective-permute-start(bf16[128,16,128]{2,1,0:T(8,128)(2,1)} %get-tuple-element.15.q0), channel_id=1, source_target_pairs={{0,4},{1,17},{2,6},{3,19},{4,0},{5,21},{6,2},{7,23},{8,12},{9,25},... | collective-permute-start | bytes 1572872 | tf_op jit(solution)/shard_map/ppermute | solution.py:345
  108.2 14.6 %collective-permute-start = (bf16[128,16,128]{2,1,0:T(8,128)(2,1)}, bf16[128,16,128]{2,1,0:T(8,128)(2,1)S(1)}, u32[]{:S(2)}, u32[]{:S(2)}) collective-permute-start(bf16[128,16,128]{2,1,0:T(8,128)(2,1)} %get-tuple-element.15.q0), channel_id=1, source_target_pairs={{0,2},{1,9},{2,4},{3,11},{4,6},{5,13},{6,0},{7,15},{8,10},{9,17},{... | collective-permute-start | bytes 1572872 | tf_op jit(solution)/shard_map/ppermute | solution.py:345
  122.8 11.2 %collective-permute-start.3 = (bf16[128,16,128]{2,1,0:T(8,128)(2,1)S(1)}, bf16[128,16,128]{2,1,0:T(8,128)(2,1)S(1)}, u32[]{:S(2)}, u32[]{:S(2)}) collective-permute-start(bf16[128,16,128]{2,1,0:T(8,128)(2,1)S(1)} %copy-done.3), channel_id=1, source_target_pairs={{0,1},{1,0},{2,3},{3,2},{4,5},{5,4},{6,7},{7,6},{8,9},{9,8},{10,11... | collective-permute-start | bytes 1572872 | tf_op jit(solution)/shard_map/ppermute | solution.py:348
  124.7 9.3 %collective-permute-start.4 = (bf16[128,16,128]{2,1,0:T(8,128)(2,1)S(1)}, bf16[128,16,128]{2,1,0:T(8,128)(2,1)S(1)}, u32[]{:S(2)}, u32[]{:S(2)}) collective-permute-start(bf16[128,16,128]{2,1,0:T(8,128)(2,1)S(1)} %collective-permute-done.q1), channel_id=1, source_target_pairs={{0,1},{1,0},{2,3},{3,2},{4,5},{5,4},{6,7},{7,6},{8,9},{9,8},{10,11... | collective-permute-start | bytes 1572872 | tf_op jit(solution)/shard_map/ppermute | solution.py:348
  124.7 9.3 %collective-permute-start.5 = (bf16[128,16,128]{2,1,0:T(8,128)(2,1)S(1)}, bf16[128,16,128]{2,1,0:T(8,128)(2,1)S(1)}, u32[]{:S(2)}, u32[]{:S(2)}) collective-permute-start(bf16[128,16,128]{2,1,0:T(8,128)(2,1)S(1)} %collective-permute-done.1.q2), channel_id=1, source_target_pairs={{0,1},{1,0},{2,3},{3,2},{4,5},{5,4},{6,7},{7,6},{8,9},{9,8},{10,11... | collective-permute-start | bytes 1572872 | tf_op jit(solution)/shard_map/ppermute | solution.py:348
  125.2 8.8 %collective-permute-start.6 = (bf16[128,16,128]{2,1,0:T(8,128)(2,1)S(1)}, bf16[128,16,128]{2,1,0:T(8,128)(2,1)S(1)}, u32[]{:S(2)}, u32[]{:S(2)}) collective-permute-start(bf16[128,16,128]{2,1,0:T(8,128)(2,1)S(1)} %collective-permute-done.2.q3), channel_id=1, source_target_pairs={{0,1},{1,0},{2,3},{3,2},{4,5},{5,4},{6,7},{7,6},{8,9},{9,8},{10,11... | collective-permute-start | bytes 1572872 | tf_op jit(solution)/shard_map/ppermute | solution.py:348
